TPU v7x, 32 devices: a whole 2x2x4 slice. The times are simulated.
32 devices in a mesh: gx: 4 (over y, x), gy: 2 (over core), vert: 4 (over z).
Axes of the slice: x: 2, y: 2, z: 4, core: 2. Of those that a mesh axis runs over, the one named last changes fastest.
Arguments:
- distribution: float32 [256, 64, 4096], P('gx', 'gy', 'vert'), as said below
- solid_mask: int32 [256, 64], P('gx', 'gy'), may hold values from 0 to 1, as said below
- normal_code: int32 [256, 64], P('gx', 'gy'), may hold values from 0 to 3
Outputs:
- new_field: float32 [256, 64, 4096], P('gx', 'gy', 'vert')
Inputs may be any that keep to these rules, and one draw needn't show every extreme that they name: distribution is positive. `solid_mask`: no solid cell lies in the first or last row or column of an aligned block of 64 x 32 cells.
All inputs are finite; a program needn't handle non-finite values.
Results may differ from a plain program's by a relative error of at most 0.0001.
Values sent between devices are 32-bit elements; how exact they have to be, the bound alone decides.
A program may use at most 128 MiB of HBM per device.

v0:
```python
import math

import jax
import jax.numpy as jnp
from jax import lax
from jax.sharding import PartitionSpec as P

NVEL = 16
STEPS = 3
NV = 4096


velocity_span = 12.0
courant = 0.08
collision_rate_inverse_tau = 2.0
wall_heat_level = 3.0


def extended(block, sides, width):
    for axis, dim in sides:
        count = lax.axis_size(axis)
        forward = [(i, i + 1) for i in range(count - 1)]
        forward.append((count - 1, 0))
        backward = [(target, source) for source, target in forward]
        low = lax.ppermute(
            lax.slice_in_dim(block, block.shape[dim] - width, None, axis=dim), axis, forward
        )
        high = lax.ppermute(lax.slice_in_dim(block, 0, width, axis=dim), axis, backward)
        block = jnp.concatenate([low, block, high], axis=dim)
    return block


def velocity_parts(vel_index, discrete_speed_total):
    mesh_step_width = velocity_span / discrete_speed_total
    centre = (discrete_speed_total - 1) / 2.0
    plane_z = vel_index // (discrete_speed_total * discrete_speed_total)
    plane_x = vel_index // discrete_speed_total % discrete_speed_total
    plane_y = vel_index % discrete_speed_total
    return (
        (plane_x.astype(jnp.float32) - centre) * mesh_step_width,
        (plane_y.astype(jnp.float32) - centre) * mesh_step_width,
        (plane_z.astype(jnp.float32) - centre) * mesh_step_width,
    )


def wall_shape(
    discrete_speed_east, discrete_speed_north, discrete_speed_upward, discrete_speed_total
):
    mesh_step_width = velocity_span / discrete_speed_total
    normalising_coefficient = mesh_step_width**3 * (2.0 * math.pi * wall_heat_level) ** (-1.5)
    return normalising_coefficient * jnp.exp(
        -(
            discrete_speed_east * discrete_speed_east
            + discrete_speed_north * discrete_speed_north
            + discrete_speed_upward * discrete_speed_upward
        )
        / (2.0 * wall_heat_level)
    )


def wall_weights(discrete_speed_east, discrete_speed_north):
    return jnp.stack(
        [
            jnp.maximum(-discrete_speed_east, 0.0),
            jnp.maximum(discrete_speed_east, 0.0),
            jnp.maximum(-discrete_speed_north, 0.0),
            jnp.maximum(discrete_speed_north, 0.0),
        ],
        axis=1,
    )


def moment_table(discrete_speed_east, discrete_speed_north, discrete_speed_upward):
    return jnp.stack(
        [
            jnp.ones_like(discrete_speed_east),
            discrete_speed_east,
            discrete_speed_north,
            discrete_speed_upward,
            discrete_speed_east * discrete_speed_east
            + discrete_speed_north * discrete_speed_north
            + discrete_speed_upward * discrete_speed_upward,
        ],
        axis=1,
    )


def neighbor_flux(partial_value, normal_code):
    from_plus_x = jnp.roll(partial_value[:, :, 0], -1, axis=0)
    from_minus_x = jnp.roll(partial_value[:, :, 1], 1, axis=0)
    from_plus_y = jnp.roll(partial_value[:, :, 2], -1, axis=1)
    from_minus_y = jnp.roll(partial_value[:, :, 3], 1, axis=1)
    return jnp.where(
        normal_code == 0,
        from_plus_x,
        jnp.where(
            normal_code == 1, from_minus_x, jnp.where(normal_code == 2, from_plus_y, from_minus_y)
        ),
    )


def transport(
    center, left_side, right_side, down_side, up_side, discrete_speed_east, discrete_speed_north
):
    return center - courant * (
        jnp.maximum(discrete_speed_east, 0.0) * (center - left_side)
        + jnp.minimum(discrete_speed_east, 0.0) * (right_side - center)
        + jnp.maximum(discrete_speed_north, 0.0) * (center - down_side)
        + jnp.minimum(discrete_speed_north, 0.0) * (up_side - center)
    )


def relax_cells(
    moved,
    aggregated_integrals,
    discrete_speed_east,
    discrete_speed_north,
    discrete_speed_upward,
    discrete_speed_total,
):
    particle_concentration = aggregated_integrals[:, 0:1]
    mean_drift_east = aggregated_integrals[:, 1:2] / particle_concentration
    mean_drift_north = aggregated_integrals[:, 2:3] / particle_concentration
    mean_drift_upward = aggregated_integrals[:, 3:4] / particle_concentration
    site_heat_level = (
        aggregated_integrals[:, 4:5] / particle_concentration
        - (
            mean_drift_east * mean_drift_east
            + mean_drift_north * mean_drift_north
            + mean_drift_upward * mean_drift_upward
        )
    ) / 3.0
    mesh_step_width = velocity_span / discrete_speed_total
    offset_x = discrete_speed_east - mean_drift_east
    offset_y = discrete_speed_north - mean_drift_north
    offset_z = discrete_speed_upward - mean_drift_upward
    maxwellian_width_sigma = offset_x * offset_x + offset_y * offset_y + offset_z * offset_z
    maxwellian_target = (
        particle_concentration
        * mesh_step_width**3
        * (2.0 * math.pi * site_heat_level) ** (-1.5)
        * jnp.exp(-maxwellian_width_sigma / (2.0 * site_heat_level))
    )
    collision_decay_factor = (
        collision_rate_inverse_tau
        * particle_concentration
        / discrete_speed_total**3
        * site_heat_level**0.28
    )
    return (moved + collision_decay_factor * maxwellian_target) / (1.0 + collision_decay_factor)


def on_device(distribution, solid_mask, normal_code):
    row_count, col_count, vel_block = distribution.shape
    flat_cells = row_count * col_count
    vel_index = lax.axis_index("vert") * vel_block + jnp.arange(vel_block, dtype=jnp.int32)
    discrete_speed_east, discrete_speed_north, discrete_speed_upward = velocity_parts(
        vel_index, NVEL
    )
    full_index = jnp.arange(NV, dtype=jnp.int32)
    full_x, full_y, full_z = velocity_parts(full_index, NVEL)
    wall_norm = jnp.sum(wall_shape(full_x, full_y, full_z, NVEL) * jnp.maximum(full_x, 0.0))
    shape_local = wall_shape(discrete_speed_east, discrete_speed_north, discrete_speed_upward, NVEL)
    weights = wall_weights(discrete_speed_east, discrete_speed_north)
    table_local = moment_table(discrete_speed_east, discrete_speed_north, discrete_speed_upward)
    is_solid = solid_mask == 1
    for time_step in range(STEPS):
        partial_value = jnp.dot(
            distribution.reshape(flat_cells, vel_block), weights, precision=lax.Precision.HIGHEST
        ).reshape(row_count, col_count, 4)
        picked = jnp.where(is_solid, neighbor_flux(partial_value, normal_code), 0.0)
        incoming = lax.psum(picked, "vert")
        ghost_value = (incoming / wall_norm)[:, :, None] * shape_local
        ghosted = jnp.where(is_solid[:, :, None], ghost_value, distribution)
        padded = extended(ghosted, (("gx", 0), ("gy", 1)), 1)
        moved = transport(
            padded[1:-1, 1:-1],
            padded[:-2, 1:-1],
            padded[2:, 1:-1],
            padded[1:-1, :-2],
            padded[1:-1, 2:],
            discrete_speed_east,
            discrete_speed_north,
        )
        flat_moved = moved.reshape(flat_cells, vel_block)
        partial_moments = jnp.dot(flat_moved, table_local, precision=lax.Precision.HIGHEST)
        aggregated_integrals = lax.psum(partial_moments, "vert")
        relaxed = relax_cells(
            flat_moved,
            aggregated_integrals,
            discrete_speed_east,
            discrete_speed_north,
            discrete_speed_upward,
            NVEL,
        ).reshape(row_count, col_count, vel_block)
        distribution = jnp.where(is_solid[:, :, None], ghost_value, relaxed)
    return distribution


def solution(mesh):
    placed = (P("gx", "gy", "vert"), P("gx", "gy"), P("gx", "gy"))
    return jax.shard_map(
        on_device, mesh=mesh, in_specs=placed, out_specs=P("gx", "gy", "vert"), check_vma=False
    )
```

profile of v0, /device:TPU:0, one launch (start us, length us, event | category | flops | bytes accessed | tf_op | source)
XLA Modules:
  0.0 368.5 jit_solution(12472584337203047156)
XLA Ops:
  0.9 9.2 %convolution_bitcast_fusion = f32[2048,4]{0,1:T(4,128)S(1)} fusion(f32[2048,1024]{1,0:T(8,128)} %bitcast.82, f32[1024,1]{0,1:T(1,128)S(1)} %get-tuple-element.97, f32[1024,1]{0,1:T(1,128)S(1)} %get-tuple-element.93, f32[1024,1]{0,1:T(1,128)S(1)} %get-tuple-element.98, f32[1024,1]{0,1:T(1,128)S(1)} %get-tuple-element.94), kind=kOutput, calls=%fused_computation.69 | convolution fusion | flops 100675584 | bytes 8437760 | tf_op jit(solution)/shard_map/dot_general | solution.py:168
  10.6 20.8 %psum.42 = f32[64,32]{1,0:T(8,128)S(1)} all-reduce(f32[64,32]{1,0:T(8,128)S(1)} %get-tuple-element.38), channel_id=1, replica_groups=mesh['gx'=4,'gy'=2,'vert'=4] {'vert'}, use_global_device_ids=true, to_apply=%region_0.1 | all-reduce | flops 2048 | bytes 16384 | tf_op jit(solution)/shard_map/psum | solution.py:172
  32.2 4.0 %multiply_select_fusion.5 = f32[64,32,1024]{2,1,0:T(8,128)S(1)} fusion(f32[64,32,1024]{2,1,0:T(8,128)} %param.3, f32[1024]{0:T(1024)S(1)} %exponential_multiply_fusion, f32[64,32]{1,0:T(8,128)S(1)} %broadcast_divide_fusion.2, pred[64,32]{1,0:T(8,128)(4,1)S(1)} %get-tuple-element.42), kind=kLoop, calls=%fused_computation.5 | loop fusion | flops 4194304 | bytes 16791552 | tf_op jit(solution)/shard_map/jit(_where)/select_n | solution.py:174
  37.7 1.6 collective-permute-start.1
  39.5 2.6 collective-permute-done
  46.6 15.7 %fusion.30 = f32[64,32,1024]{2,1,0:T(8,128)S(1)} fusion(f32[64,32,1024]{2,1,0:T(8,128)} %copy-done, f32[66,1,1024]{2,1,0:T(1,128)S(1)} %copy.108, f32[1,32,1024]{2,1,0:T(8,128)S(1)} %collective-permute-done.1, f32[1,32,1024]{2,1,0:T(8,128)S(1)} %collective-permute-done, f32[66,1,1024]{2,1,0:T(1,128)S(1)} %copy.106, f32[1024]{0:T(1024)S(1)} %get-tuple-element.88, ...), kind=kLoop, calls=%fused_computation.53 | loop fusion | flops 44040192 | bytes 17596416 | tf_op jit(solution)/shard_map/sub | solution.py:105
  62.3 7.2 %fusion.125 = f32[2048,5]{0,1:T(8,128)S(1)} fusion(f32[2048,1024]{1,0:T(8,128)S(1)} %bitcast.84, f32[1024,5]{0,1:T(8,128)S(1)} %stack.5), kind=kOutput, calls=%fused_computation.263 | convolution fusion | flops 125829120 | bytes 8450048 | tf_op jit(solution)/shard_map/dot_general | solution.py:186
  69.5 16.6 %psum.43 = f32[2048,5]{0,1:T(8,128)S(1)} all-reduce(f32[2048,5]{0,1:T(8,128)S(1)} %fusion.125), channel_id=1, replica_groups=mesh['gx'=4,'gy'=2,'vert'=4] {'vert'}, use_global_device_ids=true, to_apply=%region_2.3 | all-reduce | flops 10240 | bytes 81920 | tf_op jit(solution)/shard_map/psum | solution.py:187
  88.5 38.2 %fusion.72 = f32[64,32,4]{1,2,0:T(4,128)S(1)} fusion(f32[1024,1]{0,1:T(1,128)S(1)} %get-tuple-element.97, f32[1024,1]{0,1:T(1,128)S(1)} %get-tuple-element.93, f32[1024,1]{0,1:T(1,128)S(1)} %get-tuple-element.98, f32[1024,1]{0,1:T(1,128)S(1)} %get-tuple-element.94, f32[64,32]{1,0:T(8,128)S(1)} %div.236, f32[64,32]{1,0:T(8,128)S(1)} %div.233, ...), kind=kOutput, calls=%fused_computation.142 | convolution fusion | flops 178270208 | bytes 9340928 | tf_op jit(solution)/shard_map/dot_general | solution.py:168
  127.1 17.5 %psum.44 = f32[64,32]{1,0:T(8,128)S(1)} all-reduce(f32[64,32]{1,0:T(8,128)S(1)} %fusion.44), channel_id=1, replica_groups=mesh['gx'=4,'gy'=2,'vert'=4] {'vert'}, use_global_device_ids=true, to_apply=%region_3.4 | all-reduce | flops 2048 | bytes 16384 | tf_op jit(solution)/shard_map/psum | solution.py:172
  145.3 24.2 %multiply_select_fusion.3 = f32[64,32,1024]{2,1,0:T(8,128)S(1)} fusion(f32[64,32]{1,0:T(8,128)S(1)} %broadcast_divide_fusion.1, f32[1024]{0:T(1024)S(1)} %exponential_multiply_fusion, pred[64,32]{1,0:T(8,128)(4,1)S(1)} %get-tuple-element.42, f32[64,32]{1,0:T(8,128)S(1)} %div.236, f32[64,32]{1,0:T(8,128)S(1)} %div.233, f32[64,32]{1,0:T(8,128)S(1)} %sub.264, ...), kind=kLoop, calls=%fused_computation.3 | loop fusion | flops 81788928 | bytes 17688576 | tf_op jit(solution)/shard_map/jit(_where)/select_n | solution.py:174
  169.6 1.7 collective-permute-start.4
  172.8 2.7 collective-permute-done.4
  179.5 8.0 %fusion.17 = f32[64,32,1024]{2,1,0:T(8,128)S(1)} fusion(f32[64,32,1024]{2,1,0:T(8,128)S(1)} %multiply_select_fusion.3, f32[66,1,1024]{2,1,0:T(1,128)S(1)} %copy.115, f32[1,32,1024]{2,1,0:T(8,128)S(1)} %collective-permute-done.5, f32[1,32,1024]{2,1,0:T(8,128)S(1)} %collective-permute-done.4, f32[66,1,1024]{2,1,0:T(1,128)S(1)} %copy.113, ...), kind=kLoop, calls=%fused_computation.32 | loop fusion | flops 44040192 | bytes 17596416 | tf_op jit(solution)/shard_map/sub | solution.py:105
  187.5 7.2 %fusion.126 = f32[2048,5]{0,1:T(8,128)S(1)} fusion(f32[2048,1024]{1,0:T(8,128)S(1)} %bitcast.85, f32[1024,5]{0,1:T(8,128)S(1)} %stack.5), kind=kOutput, calls=%fused_computation.264 | convolution fusion | flops 125829120 | bytes 8450048 | tf_op jit(solution)/shard_map/dot_general | solution.py:186
  194.7 17.1 %psum.45 = f32[2048,5]{0,1:T(8,128)S(1)} all-reduce(f32[2048,5]{0,1:T(8,128)S(1)} %fusion.126), channel_id=1, replica_groups=mesh['gx'=4,'gy'=2,'vert'=4] {'vert'}, use_global_device_ids=true, to_apply=%region_4.5 | all-reduce | flops 10240 | bytes 81920 | tf_op jit(solution)/shard_map/psum | solution.py:187
  213.7 38.2 %fusion.70 = f32[64,32,4]{1,2,0:T(4,128)S(1)} fusion(f32[1024,1]{0,1:T(1,128)S(1)} %get-tuple-element.97, f32[1024,1]{0,1:T(1,128)S(1)} %get-tuple-element.93, f32[1024,1]{0,1:T(1,128)S(1)} %get-tuple-element.98, f32[1024,1]{0,1:T(1,128)S(1)} %get-tuple-element.94, f32[64,32]{1,0:T(8,128)S(1)} %div.249, f32[64,32]{1,0:T(8,128)S(1)} %div.246, ...), kind=kOutput, calls=%fused_computation.140 | convolution fusion | flops 178270208 | bytes 9340928 | tf_op jit(solution)/shard_map/dot_general | solution.py:168
  252.3 17.3 %psum.46 = f32[64,32]{1,0:T(8,128)S(1)} all-reduce(f32[64,32]{1,0:T(8,128)S(1)} %fusion.45), channel_id=1, replica_groups=mesh['gx'=4,'gy'=2,'vert'=4] {'vert'}, use_global_device_ids=true, to_apply=%region_5.6 | all-reduce | flops 2048 | bytes 16384 | tf_op jit(solution)/shard_map/psum | solution.py:172
  270.3 24.2 %multiply_select_fusion.1 = f32[64,32,1024]{2,1,0:T(8,128)S(1)} fusion(f32[64,32]{1,0:T(8,128)S(1)} %broadcast_divide_fusion, f32[1024]{0:T(1024)S(1)} %exponential_multiply_fusion, pred[64,32]{1,0:T(8,128)(4,1)S(1)} %get-tuple-element.42, f32[64,32]{1,0:T(8,128)S(1)} %div.249, f32[64,32]{1,0:T(8,128)S(1)} %div.246, f32[64,32]{1,0:T(8,128)S(1)} %sub.279, ...), kind=kLoop, calls=%fused_computation.1 | loop fusion | flops 81788928 | bytes 17688576 | tf_op jit(solution)/shard_map/jit(_where)/select_n | solution.py:174
  297.8 2.8 collective-permute-done.8
  304.4 8.0 %fusion.4 = f32[64,32,1024]{2,1,0:T(8,128)S(1)} fusion(f32[64,32,1024]{2,1,0:T(8,128)S(1)} %multiply_select_fusion.1, f32[66,1,1024]{2,1,0:T(1,128)S(1)} %copy.123, f32[1,32,1024]{2,1,0:T(8,128)S(1)} %collective-permute-done.9, f32[1,32,1024]{2,1,0:T(8,128)S(1)} %collective-permute-done.8, f32[66,1,1024]{2,1,0:T(1,128)S(1)} %copy.121, ...), kind=kLoop, calls=%fused_computation.11 | loop fusion | flops 44040192 | bytes 17596416 | tf_op jit(solution)/shard_map/sub | solution.py:105
  312.5 7.2 %fusion.127 = f32[2048,5]{0,1:T(8,128)S(1)} fusion(f32[2048,1024]{1,0:T(8,128)S(1)} %bitcast.83, f32[1024,5]{0,1:T(8,128)S(1)} %stack.5), kind=kOutput, calls=%fused_computation.265 | convolution fusion | flops 125829120 | bytes 8450048 | tf_op jit(solution)/shard_map/dot_general | solution.py:186
  319.7 16.9 %psum.47 = f32[2048,5]{0,1:T(8,128)S(1)} all-reduce(f32[2048,5]{0,1:T(8,128)S(1)} %fusion.127), channel_id=1, replica_groups=mesh['gx'=4,'gy'=2,'vert'=4] {'vert'}, use_global_device_ids=true, to_apply=%region_6.7 | all-reduce | flops 10240 | bytes 81920 | tf_op jit(solution)/shard_map/psum | solution.py:187
  338.4 29.9 %multiply_select_fusion = f32[64,32,1024]{2,1,0:T(8,128)} fusion(f32[64,32]{1,0:T(8,128)S(1)} %div.262, f32[64,32]{1,0:T(8,128)S(1)} %div.259, f32[64,32]{1,0:T(8,128)S(1)} %sub.294, f32[64,32]{1,0:T(8,128)S(1)} %sub.291, f32[64,32]{1,0:T(8,128)S(1)} %sub.288, f32[64,32]{1,0:T(8,128)S(1)} %mul.591, f32[64,32]{1,0:T(8,128)S(1)} %mul.586, ...), kind=kLoop, calls=%fused_computation | loop fusion | flops 77594624 | bytes 17680384 | tf_op jit(solution)/shard_map/jit(_where)/select_n | solution.py:196
  (118 shorter events, 28.9 us)
Async XLA Ops:
  0.0 10.2 %copy-start.3 = (s32[64,32]{0,1:T(8,128)S(1)}, s32[64,32]{0,1:T(8,128)}, u32[]{:S(2)}) copy-start(s32[64,32]{0,1:T(8,128)} %param.4) | copy-start | bytes 24580
  0.0 10.3 %copy-start.4 = (s32[64,32]{0,1:T(8,128)S(1)}, s32[64,32]{0,1:T(8,128)}, u32[]{:S(2)}) copy-start(s32[64,32]{0,1:T(8,128)} %param.5) | copy-start | bytes 24580
  36.1 7.4 %copy-start = (f32[64,32,1024]{2,1,0:T(8,128)}, f32[64,32,1024]{2,1,0:T(8,128)S(1)}, u32[]{:S(2)}) copy-start(f32[64,32,1024]{2,1,0:T(8,128)S(1)} %multiply_select_fusion.5) | copy-start | bytes 25165828
  36.2 5.9 %collective-permute-start = (f32[1,32,1024]{2,1,0:T(8,128)S(1)}, f32[1,32,1024]{2,1,0:T(8,128)S(1)}, u32[]{:S(2)}, u32[]{:S(2)}) collective-permute-start(f32[1,32,1024]{2,1,0:T(8,128)S(1)} %get-tuple-element.53), channel_id=1, source_target_pairs={{0,8},{8,16},{16,24},{24,0},{1,9},{9,17},{17,25},{25,1},{2,10},{10... | collective-permute-start | bytes 393224 | tf_op jit(solution)/shard_map/ppermute | solution.py:25
  37.7 5.8 %collective-permute-start.1 = (f32[1,32,1024]{2,1,0:T(8,128)S(1)}, f32[1,32,1024]{2,1,0:T(8,128)S(1)}, u32[]{:S(2)}, u32[]{:S(2)}) collective-permute-start(f32[1,32,1024]{2,1,0:T(8,128)S(1)} %get-tuple-element.54), channel_id=1, source_target_pairs={{8,0},{16,8},{24,16},{0,24},{9,1},{17,9},{25,17},{1,25},{10,2},{18... | collective-permute-start | bytes 393224 | tf_op jit(solution)/shard_map/ppermute | solution.py:28
  44.2 1.6 collective-permute-start.3
  44.3 2.0 collective-permute-start.2
  169.5 18.0 %copy-start.1 = (f32[64,32,1024]{2,1,0:T(8,128)}, f32[64,32,1024]{2,1,0:T(8,128)S(1)}, u32[]{:S(2)}) copy-start(f32[64,32,1024]{2,1,0:T(8,128)S(1)} %multiply_select_fusion.3) | copy-start | bytes 25165828
  169.6 5.9 %collective-permute-start.4 = (f32[1,32,1024]{2,1,0:T(8,128)S(1)}, f32[1,32,1024]{2,1,0:T(8,128)S(1)}, u32[]{:S(2)}, u32[]{:S(2)}) collective-permute-start(f32[1,32,1024]{2,1,0:T(8,128)S(1)} %get-tuple-element.51), channel_id=1, source_target_pairs={{0,8},{8,16},{16,24},{24,0},{1,9},{9,17},{17,25},{25,1},{2,10},{10... | collective-permute-start | bytes 393224 | tf_op jit(solution)/shard_map/ppermute | solution.py:25
  171.3 5.2 %collective-permute-start.5 = (f32[1,32,1024]{2,1,0:T(8,128)S(1)}, f32[1,32,1024]{2,1,0:T(8,128)S(1)}, u32[]{:S(2)}, u32[]{:S(2)}) collective-permute-start(f32[1,32,1024]{2,1,0:T(8,128)S(1)} %get-tuple-element.52), channel_id=1, source_target_pairs={{8,0},{16,8},{24,16},{0,24},{9,1},{17,9},{25,17},{1,25},{10,2},{18... | collective-permute-start | bytes 393224 | tf_op jit(solution)/shard_map/ppermute | solution.py:28
  177.1 1.6 collective-permute-start.7
  177.3 1.9 collective-permute-start.6
  294.6 17.9 %copy-start.2 = (f32[64,32,1024]{2,1,0:T(8,128)}, f32[64,32,1024]{2,1,0:T(8,128)S(1)}, u32[]{:S(2)}) copy-start(f32[64,32,1024]{2,1,0:T(8,128)S(1)} %multiply_select_fusion.1) | copy-start | bytes 25165828
  294.6 5.9 %collective-permute-start.8 = (f32[1,32,1024]{2,1,0:T(8,128)S(1)}, f32[1,32,1024]{2,1,0:T(8,128)S(1)}, u32[]{:S(2)}, u32[]{:S(2)}) collective-permute-start(f32[1,32,1024]{2,1,0:T(8,128)S(1)} %get-tuple-element.49), channel_id=1, source_target_pairs={{0,8},{8,16},{16,24},{24,0},{1,9},{9,17},{17,25},{25,1},{2,10},{10... | collective-permute-start | bytes 393224 | tf_op jit(solution)/shard_map/ppermute | solution.py:25
  296.2 5.3 %collective-permute-start.9 = (f32[1,32,1024]{2,1,0:T(8,128)S(1)}, f32[1,32,1024]{2,1,0:T(8,128)S(1)}, u32[]{:S(2)}, u32[]{:S(2)}) collective-permute-start(f32[1,32,1024]{2,1,0:T(8,128)S(1)} %get-tuple-element.50), channel_id=1, source_target_pairs={{8,0},{16,8},{24,16},{0,24},{9,1},{17,9},{25,17},{1,25},{10,2},{18... | collective-permute-start | bytes 393224 | tf_op jit(solution)/shard_map/ppermute | solution.py:28
  302.1 1.6 collective-permute-start.11
  302.2 1.9 collective-permute-start.10
where the time goes:
time: 372 us; the launch traced here: 368 us
  other arithmetic  123 us (33%)
  matrix products  107 us (29%)
  blocking collectives  106 us (28%)
  waiting for transfers between devices  14.8 us (4%)
  starting transfers between devices  11.3 us (3%)
  local copies, waits for them, and re-layouts  5.06 us (1%)
    dot_general x3, matrix products, on_device(): jnp.dot(distribution.reshape(flat_cells, vel_block), weights, precision=l...  85.5 us
    psum x3, blocking collectives, on_device(): incoming = lax.psum(picked, 'vert')  55.7 us
    select_n x3, other arithmetic, on_device(): ghosted = jnp.where(is_solid[:, :, None], ghost_value, distribution)  52.4 us
    psum x3, blocking collectives, on_device(): aggregated_integrals = lax.psum(partial_moments, 'vert')  50.5 us
    sub x3, other arithmetic, transport(): center - courant * (jnp.maximum(discrete_speed_east, 0.0) * (center - lef...  31.8 us
    select_n x1, other arithmetic, on_device(): distribution = jnp.where(is_solid[:, :, None], ghost_value, relaxed)  29.9 us
    dot_general x3, matrix products, on_device(): jnp.dot(flat_moved, table_local, precision=lax.Precision.HIGHEST)  21.5 us
    ppermute x6, waiting for transfers between devices, extended(): lax.ppermute(lax.slice_in_dim(block, block.shape[dim] - width, None, axis...  8.54 us
  transfers between devices with their start and end apart: 12, of which 12 were waited for; matrix products, arithmetic and copies ran while one was open for 0% of the time, Pallas kernels for 0%

commit v1 on v0

v1 whole, which is shorter than its diff:
```python
import functools
import math

import jax
import jax.numpy as jnp
import ml_dtypes
import numpy as np
from jax import lax
from jax.experimental import pallas as pl
from jax.experimental.pallas import tpu as pltpu
from jax.sharding import PartitionSpec as P

NVEL = 16
STEPS = 3
SPAN = 12.0
COURANT = 0.08
INV_TAU = 2.0
WALL_T = 3.0
PLANE = NVEL * NVEL
LANES = 128
H = SPAN / NVEL
MESH = pl.DeviceIdType.MESH
F32 = jnp.float32
BF16 = jnp.bfloat16
HALVES = PLANE // LANES


def split3(x):
    x = np.asarray(x, np.float64)
    pieces = []
    for _ in range(3):
        piece = x.astype(np.float32).astype(ml_dtypes.bfloat16)
        pieces.append(piece)
        x = x - piece.astype(np.float64)
    return pieces


def tables(nz):
    axis = (np.arange(NVEL) - (NVEL - 1) / 2.0) * H
    vx = np.repeat(axis, NVEL)
    vy = np.tile(axis, NVEL)
    zloc = (np.arange(nz) - (nz - 1) / 2.0) * H
    lx, ly, lz = np.tile(vx, nz), np.tile(vy, nz), np.repeat(zloc, PLANE)

    def five(x, y, z):
        return [np.ones_like(x), x, y, z, x * x + y * y + z * z]

    def sides(x, y):
        return [np.maximum(x, 0), np.maximum(-x, 0), np.maximum(y, 0), np.maximum(-y, 0)]

    weight = np.zeros((40, nz * PLANE))
    for g, factor in enumerate([np.ones_like(lx)] + sides(lx, ly)):
        for r, phi in enumerate(five(lx, ly, lz)):
            weight[8 * g + r] = factor * phi
    w = np.concatenate(split3(weight), axis=0)

    norm = H**3 * (2 * math.pi * WALL_T) ** -1.5
    fx, fy, fz = np.tile(vx, NVEL), np.tile(vy, NVEL), np.repeat(axis, PLANE)
    shape = norm * np.exp(-(fx**2 + fy**2 + fz**2) / (2 * WALL_T))
    wall_norm = float(np.sum(shape * np.maximum(fx, 0)))
    wall = [
        [COURANT * float(np.sum(shape * s * phi)) for s in sides(fx, fy)]
        for phi in five(fx, fy, fz)
    ]

    cols = 2 + nz + 1 + 2
    b = np.zeros((16, cols * LANES))
    sxy = norm * np.exp(-(vx**2 + vy**2) / (2 * WALL_T))
    for half in range(2):
        ln = slice(half * LANES, (half + 1) * LANES)
        hx, hy = vx[ln], vy[ln]
        b[0, ln], b[1, ln], b[2, ln], b[3, ln] = 1.0, hx, hy, hx**2 + hy**2
        at = (3 + nz + half) * LANES
        to = slice(at, at + LANES)
        b[5 + nz, to] = COURANT * np.maximum(hx, 0) * sxy[ln]
        b[6 + nz, to] = COURANT * np.maximum(-hx, 0) * sxy[ln]
        b[7 + nz, to] = COURANT * np.maximum(hy, 0) * sxy[ln]
        b[8 + nz, to] = COURANT * np.maximum(-hy, 0) * sxy[ln]
    for z in range(nz + 1):
        b[4 + z, (2 + z) * LANES : (3 + z) * LANES] = 1.0
    bh, bm, bl = split3(b)
    bst = np.concatenate([bh, bm, bh, bl, bm, bh], axis=0)

    vec = np.zeros((8, LANES), np.float32)
    for half in range(2):
        ln = slice(half * LANES, (half + 1) * LANES)
        vec[half] = 1 - COURANT * (np.abs(vx[ln]) + np.abs(vy[ln]))
        vec[2 + half] = COURANT * np.abs(vx[ln])
    vec[4] = COURANT * np.abs(vy[:LANES])
    vec[5] = vy[:LANES] > 0
    return w, bst, vec, wall_norm, wall, norm


def kernel(
    cfg, f_hbm, masks, w_ref, b_ref, vec, out_hbm,
    fa, fb, bc, q, qy, qx, a_ref, r_ref, p_ref, pst, hs, hr, hb, wold,
    lsem, osem, zss, zrs, xss, xrs, hss, hrs, qyss, qyrs, qxss, qxrs,
):
    rows, cols, nz, nx, ny, nv, wall_norm, wall, norm = cfg
    cells = rows * cols
    chunk = 8
    cc = chunk * cols
    nch = rows // chunk
    gx, gy, vt = lax.axis_index("gx"), lax.axis_index("gy"), lax.axis_index("vert")
    right, left = {"gx": lax.rem(gx + 1, nx)}, {"gx": lax.rem(gx + nx - 1, nx)}
    across = [{"gy": lax.rem(gy + 1, ny)}]
    if ny > 2:
        across.append({"gy": lax.rem(gy + ny - 1, ny)})
    peers = [{"vert": lax.rem(vt + k, nv)} for k in range(1, nv)]

    def local_copy(k):
        return pltpu.make_async_copy(
            f_hbm.at[pl.ds(k * chunk, chunk)], fa.at[pl.ds(1 + k * chunk, chunk)], lsem.at[k]
        )

    for k in range(nch):
        local_copy(k).start()

    barrier = pltpu.get_barrier_semaphore()
    everyone = [right, left] + across + peers
    for dev in everyone:
        pl.semaphore_signal(barrier, inc=1, device_id=dev, device_id_type=MESH)
    pl.semaphore_wait(barrier, len(everyone))

    def remote(src, dst, ss, rs, dev):
        return pltpu.make_async_remote_copy(
            src_ref=src, dst_ref=dst, send_sem=ss, recv_sem=rs, device_id=dev, device_id_type=MESH
        )

    def halo_x(step, src, first, dst):
        out = []
        for z in range(nz):
            hi = pl.ds((2 * z + 1) * LANES, LANES)
            lo = pl.ds(2 * z * LANES, LANES)
            out.append(remote(src.at[first + rows - 1, :, hi], dst.at[0, :, hi],
                              xss.at[step, 0, z], xrs.at[step, 0, z], right))
            out.append(remote(src.at[first, :, lo], dst.at[rows + 1, :, lo],
                              xss.at[step, 1, z], xrs.at[step, 1, z], left))
        return out

    z0 = (vt.astype(F32) * nz + (nz - 1) / 2.0 - (NVEL - 1) / 2.0) * H
    vz = [z0 + (z - (nz - 1) / 2.0) * H for z in range(nz)]
    sz = [jnp.exp(jnp.full((1, LANES), 0.0, F32) - vz[z] * vz[z] / (2 * WALL_T)) for z in range(nz)]
    up = jnp.broadcast_to(vec[5:6, :], (8, LANES)) > 0.5
    sub = lax.broadcasted_iota(jnp.int32, (8, LANES), 0)
    edge_lo = up & (sub == 0)
    edge_hi = jnp.logical_not(up) & (sub == 7)

    def moments(x, k):
        hi = x.astype(BF16)
        lo = (x - hi.astype(F32)).astype(BF16)
        dims = (((1,), (1,)), ((), ()))
        o = lax.dot_general(w_ref[...], hi, dims, preferred_element_type=F32)
        o = o + lax.dot_general(w_ref[...], lo, dims, preferred_element_type=F32)
        at = pl.ds(pl.multiple_of(k * cc, cc), cc)
        q[:, at] = o[0:40] + o[40:80] + o[80:120]

    def pack(step, buf, k):
        for r in range(chunk):
            i = 1 + k * chunk + r
            for b in range(2 * nz):
                ln = slice(b * LANES, (b + 1) * LANES)
                hs[step, k, r : r + 1, ln] = jnp.where(
                    up[0:1], buf[i, cols - 1 : cols, ln], buf[i, 0:1, ln]
                )

    def load_chunk(k, carry):
        local_copy(k).wait()
        x = fa[pl.ds(1 + k * chunk, chunk)].reshape(cc, nz * PLANE)
        moments(x, k)
        at = pl.ds(pl.multiple_of(k * cc, cc), cc)
        ones = (lax.broadcasted_iota(jnp.int32, (8, LANES), 0) == 0).astype(BF16)
        gasb = lax.dot_general(masks[:, at].astype(BF16), ones, (((0,), (0,)), ((), ())),
                               preferred_element_type=F32)
        gasb = gasb.reshape(chunk, cols, LANES)
        for b in range(2 * nz):
            ln = slice(b * LANES, (b + 1) * LANES)
            fa[pl.ds(1 + k * chunk, chunk), :, ln] = fa[pl.ds(1 + k * chunk, chunk), :, ln] * gasb
        pack(0, fa, k)
        return carry

    xs = halo_x(0, f_hbm, 0, fa)
    for c in xs:
        c.start()
    lax.fori_loop(0, nch, load_chunk, 0)

    gas = masks[0:1, :]
    picks = [masks[1 + k : 2 + k, :] for k in range(4)]
    solid = masks[5:6, :] > 0.5
    lane = lax.broadcasted_iota(jnp.int32, (8, cells), 1)
    row8 = lax.broadcasted_iota(jnp.int32, (8, cells), 0)

    def shift(v, s):
        return pltpu.roll(v, s % cells, 1)

    wold[...] = jnp.zeros_like(wold)
    bufs = [fa, fb]
    for step in range(STEPS):
        src, dst = bufs[step % 2], bufs[(step + 1) % 2]
        last = step == STEPS - 1
        hcopy = [remote(hs.at[step], hr.at[step, n], hss.at[step, n], hrs.at[step, n], dev)
                 for n, dev in enumerate(across)]
        qcopy = [remote(q.at[pl.ds(24, 16)], qy.at[step, n], qyss.at[step, n], qyrs.at[step, n], dev)
                 for n, dev in enumerate(across)]
        qcopy += [
            remote(q.at[pl.ds(8, 8), pl.ds(cells - LANES, LANES)], qx.at[step, 0],
                   qxss.at[step, 0], qxrs.at[step, 0], right),
            remote(q.at[pl.ds(16, 8), pl.ds(0, LANES)], qx.at[step, 1],
                   qxss.at[step, 1], qxrs.at[step, 1], left),
        ]
        for c in qcopy:
            c.start()
        for c in hcopy:
            c.start()
        if step > 0:
            xs = halo_x(step, src, 1, src)
            for c in xs:
                c.start()

        xp, xm, yp, ym = (q[8 * g : 8 * g + 8, :] for g in range(1, 5))
        inc = (picks[0] * shift(xm[0:1], -cols) + picks[1] * shift(xp[0:1], cols)
               + picks[2] * shift(ym[0:1], -1) + picks[3] * shift(yp[0:1], 1))
        base = (q[0:8, :] - COURANT * (xp + xm + yp + ym)) * gas
        sxp, sxm = shift(xp * gas, cols), shift(xm * gas, -cols)
        syp, sym = shift(yp * gas, 1), shift(ym * gas, -1)
        for c in qcopy:
            c.wait()
        reps = cells // LANES
        left_in = jnp.concatenate([pltpu.roll(qx[step, 0], cols, 1)] * reps, axis=1)
        right_in = jnp.concatenate([pltpu.roll(qx[step, 1], LANES - cols, 1)] * reps, axis=1)
        sxp = jnp.where(lane < cols, left_in, sxp)
        sxm = jnp.where(lane >= cells - cols, right_in, sxm)
        col = lane % cols
        syp = jnp.where(col == 0, shift(qy[step, 0, 0:8], 1 - cols), syp)
        sym = jnp.where(col == cols - 1, shift(qy[step, len(across) - 1, 8:16], cols - 1), sym)
        part = base + COURANT * (sxp + sxm + syp + sym)
        z_row = part[3:4] + z0 * part[0:1]
        e_row = part[4:5] + 2 * z0 * part[3:4] + z0 * z0 * part[0:1]
        part = jnp.where(row8 == 3, z_row, jnp.where(row8 == 4, e_row, jnp.where(row8 == 5, inc, part)))
        a_ref[...] = part
        zc = [remote(a_ref, r_ref.at[step, k], zss.at[step, k], zrs.at[step, k], peers[k])
              for k in range(nv - 1)]
        for c in zc:
            c.start()
        for c in zc:
            c.wait()
        tot = part
        for k in range(nv - 1):
            tot = tot + r_ref[step, k]
        p_ref[0:8, :] = tot
        w = p_ref[5:6, :] * (1.0 / wall_norm)
        near = [shift(w, cols), shift(w, -cols), shift(w, 1), shift(w, -1)]
        mom = []
        for r in range(5):
            m = p_ref[r : r + 1, :]
            for d in range(4):
                if abs(wall[r][d]) > 1e-12 * abs(wall[0][0]):
                    m = m + wall[r][d] * near[d]
            mom.append(m)
        rho = mom[0]
        ux, uy, uz = mom[1] / rho, mom[2] / rho, mom[3] / rho
        temp = (mom[4] / rho - (ux * ux + uy * uy + uz * uz)) / 3.0
        rate = (INV_TAU / NVEL**3) * rho * jnp.exp(0.28 * jnp.log(temp))
        two_pi_t = (2.0 * math.pi) * temp
        amp = rate / (1.0 + rate) * rho * H**3 / (two_pi_t * jnp.sqrt(two_pi_t))
        inv = 1.0 / (1.0 + rate)
        ux, uy, uz = (jnp.where(solid, 0.0, v) for v in (ux, uy, uz))
        g = jnp.where(solid, 0.5 / WALL_T, 0.5 / temp)
        amp = jnp.where(solid, w * norm, amp)
        inv = jnp.where(solid, 0.0, inv)
        diff = w - wold[...]
        wold[...] = w
        lines = [-g * (ux * ux + uy * uy), 2 * g * ux, 2 * g * uy, -g]
        lines += [amp * jnp.exp(-g * (vz[z] - uz) * (vz[z] - uz)) for z in range(nz)]
        lines += [inv, shift(diff, cols), shift(diff, -cols), shift(diff, 1), shift(diff, -1)]
        lines += [jnp.zeros_like(inv)] * (16 - len(lines))
        for r in range(16):
            p_ref[r : r + 1, :] = lines[r]
        pv = p_ref[...]
        ph = pv.astype(BF16)
        rest = pv - ph.astype(F32)
        pm = rest.astype(BF16)
        plo = (rest - pm.astype(F32)).astype(BF16)
        for n, piece in enumerate([ph, ph, pm, ph, pm, plo]):
            pst[16 * n : 16 * n + 16, :] = piece

        for c in hcopy + xs:
            c.wait()

        def relax_row(i, rr, bcrow):
            def take(n):
                return bc[pl.ds(bcrow, cols), n * LANES : (n + 1) * LANES]

            inv_b = take(2 + nz)
            for half in range(2):
                exy = jnp.exp(take(half))
                pxy = take(3 + nz + half)
                for z in range(nz):
                    b = 2 * z + half
                    ln = slice(b * LANES, (b + 1) * LANES)
                    c = src[1 + i, :, ln]
                    r = src[i if half == 1 else i + 2, :, ln]
                    dn = pltpu.roll(c, 1, 0)
                    un = pltpu.roll(c, cols - 1, 0)
                    hrow = hb[rr, :, ln]
                    s = []
                    for t in range(cols // 8):
                        tl = slice(8 * t, 8 * t + 8)
                        v = jnp.where(up, dn[tl], un[tl])
                        if t == 0:
                            v = jnp.where(edge_lo, hrow, v)
                        if t == cols // 8 - 1:
                            v = jnp.where(edge_hi, hrow, v)
                        s.append(v)
                    s = jnp.concatenate(s, axis=0)
                    moved = c * vec[half : half + 1, :] + r * vec[2 + half : 3 + half, :] + s * vec[4:5, :]
                    dst[1 + i, :, ln] = inv_b * (moved + pxy * sz[z]) + take(2 + z) * exy

        def out_copy(k):
            return pltpu.make_async_copy(
                dst.at[pl.ds(1 + k * chunk, chunk)], out_hbm.at[pl.ds(k * chunk, chunk)], osem.at[k]
            )

        def relax_chunk(k, carry):
            at = pl.ds(pl.multiple_of(k * cc, cc), cc)
            bc[...] = lax.dot_general(pst[:, at], b_ref[...], (((0,), (0,)), ((), ())),
                                      preferred_element_type=F32)

            def one(r, c2):
                relax_row(k * chunk + r, r, pl.multiple_of(r * cols, cols))
                return c2

            for r in range(chunk):
                for b in range(2 * nz):
                    ln = slice(b * LANES, (b + 1) * LANES)
                    low = jnp.broadcast_to(hr[step, 0, k, r : r + 1, ln], (8, LANES))
                    if ny == 2:
                        hb[r, :, ln] = low
                    else:
                        high = jnp.broadcast_to(hr[step, 1, k, r : r + 1, ln], (8, LANES))
                        hb[r, :, ln] = jnp.where(up, low, high)

            lax.fori_loop(0, chunk, one, 0)
            if last:
                out_copy(k).start()
            else:
                pack(step + 1, dst, k)
                moments(dst[pl.ds(1 + k * chunk, chunk)].reshape(cc, nz * PLANE), k)
            return carry

        lax.fori_loop(0, nch, relax_chunk, 0)
        if last:
            for k in range(nch):
                out_copy(k).wait()


def solution(mesh):
    nx, ny, nv = mesh.shape["gx"], mesh.shape["gy"], mesh.shape["vert"]
    sides = 1 if ny == 2 else 2

    def on_device(f, solid_mask, normal_code):
        rows, cols, vel = f.shape
        nz = vel // PLANE
        cells = rows * cols
        w, bst, vec, wall_norm, wall, norm = tables(nz)
        sm = solid_mask.reshape(1, cells) == 1
        nc = normal_code.reshape(1, cells)
        lines = [jnp.logical_not(sm)] + [sm & (nc == k) for k in range(4)] + [sm]
        lines += [jnp.zeros_like(sm)] * 2
        masks = jnp.concatenate(lines, axis=0).astype(F32)
        cfg = (rows, cols, nz, nx, ny, nv, wall_norm, wall, norm)
        vm = pl.BlockSpec(memory_space=pltpu.VMEM)
        hbm = pl.BlockSpec(memory_space=pl.ANY)
        dma = pltpu.SemaphoreType.DMA
        bw = bst.shape[1]
        chunk = 8
        return pl.pallas_call(
            functools.partial(kernel, cfg),
            out_shape=jax.ShapeDtypeStruct(f.shape, F32),
            in_specs=[hbm, vm, vm, vm, vm],
            out_specs=hbm,
            scratch_shapes=[
                pltpu.VMEM((rows + 2, cols, vel), F32),
                pltpu.VMEM((rows + 2, cols, vel), F32),
                pltpu.VMEM((chunk * cols, bw), F32),
                pltpu.VMEM((40, cells), F32),
                pltpu.VMEM((STEPS, sides, 16, cells), F32),
                pltpu.VMEM((STEPS, 2, 8, LANES), F32),
                pltpu.VMEM((8, cells), F32),
                pltpu.VMEM((STEPS, nv - 1, 8, cells), F32),
                pltpu.VMEM((16, cells), F32),
                pltpu.VMEM((96, cells), BF16),
                pltpu.VMEM((STEPS, rows // chunk, chunk, vel), F32),
                pltpu.VMEM((STEPS, sides, rows // chunk, chunk, vel), F32),
                pltpu.VMEM((chunk, 8, vel), F32),
                pltpu.VMEM((1, cells), F32),
                dma((rows // chunk,)), dma((rows // chunk,)),
                dma((STEPS, nv - 1)), dma((STEPS, nv - 1)),
                dma((STEPS, 2, nz)), dma((STEPS, 2, nz)),
                dma((STEPS, sides)), dma((STEPS, sides)),
                dma((STEPS, sides)), dma((STEPS, sides)),
                dma((STEPS, 2)), dma((STEPS, 2)),
            ],
            compiler_params=pltpu.CompilerParams(
                collective_id=0, has_side_effects=True, vmem_limit_bytes=60 * 2**20
            ),
        )(f, masks, jnp.asarray(w), jnp.asarray(bst), jnp.asarray(vec))

    placed = (P("gx", "gy", "vert"), P("gx", "gy"), P("gx", "gy"))
    return jax.shard_map(
        on_device, mesh=mesh, in_specs=placed, out_specs=P("gx", "gy", "vert"), check_vma=False
    )
```

time: 372 us -> 86.5 us (0.23)
  other arithmetic: 123 us -> 2.15 us
  matrix products: 107 us -> 0 us
  blocking collectives: 106 us -> 0 us
  Pallas kernels: 0 us -> 74.5 us
  waiting for transfers between devices: 14.8 us -> 0 us
  starting transfers between devices: 11.3 us -> 0 us
  local copies, waits for them, and re-layouts: 5.06 us -> 9.51 us
    dot_general x6 -> x0, matrix products: 107 us -> none  [the longest x3 85.5 us: on_device(): jnp.dot(distribution.reshape(flat_cells, vel_block), weights, precision=l...]
    psum x6 -> x0, blocking collectives: 106 us -> none  [the longest x3 55.7 us: on_device(): incoming = lax.psum(picked, 'vert')]
    select_n x7 -> x0, other arithmetic: 82.6 us -> none  [the longest x3 52.4 us: on_device(): ghosted = jnp.where(is_solid[:, :, None], ghost_value, distribution)]
    pallas_call x0 -> x1, Pallas kernels: none -> 74.5 us  [on_device(): pl.pallas_call(functools.partial(kernel, cfg), out_shape=jax.ShapeDtypeSt...]
    sub x3 -> x0, other arithmetic: 31.8 us -> none  [transport(): center - courant * (jnp.maximum(discrete_speed_east, 0.0) * (center - lef...]
    ppermute x12 -> x0, waiting for transfers between devices: 14.8 us -> none  [the longest x6 8.54 us: extended(): lax.ppermute(lax.slice_in_dim(block, block.shape[dim] - width, None, axis...]
    ppermute x12 -> x0, starting transfers between devices: 11.3 us -> none  [the longest x6 6.42 us: extended(): lax.ppermute(lax.slice_in_dim(block, block.shape[dim] - width, None, axis...]
    unnamed x16 -> x1, local copies, waits for them, and re-layouts: 0.2 us -> 8.44 us
  transfers between devices with their start and end apart: 12 -> 0, of which waited for: 12 -> 0; matrix products, arithmetic and copies ran while one was open for 0% -> 0% of each run, Pallas kernels for 0% -> 0%
where the time goes in v1:
time: 86.5 us; the launch traced here: 86.2 us
  Pallas kernels  74.5 us (86%)
  local copies, waits for them, and re-layouts  9.51 us (11%)
  other arithmetic  2.15 us (2%)
    pallas_call x1, Pallas kernels, on_device(): pl.pallas_call(functools.partial(kernel, cfg), out_shape=jax.ShapeDtypeSt...  74.5 us
    unnamed x1, local copies, waits for them, and re-layouts  8.44 us

profile of v1, /device:TPU:0, one launch (start us, length us, event | category | flops | bytes accessed | tf_op | source)
XLA Modules:
  0.0 86.2 jit_solution(4476129447013803167)
XLA Ops:
  0.0 0.7 broadcast_compare_fusion.4
  0.7 0.1 copy.12
  0.8 0.1 eq.100
  0.9 0.7 broadcast_compare_fusion
  1.7 0.1 copy.16
  1.8 0.1 eq.111
  1.8 0.1 copy.14
  2.0 0.1 eq.105
  2.0 0.1 copy.13
  2.2 0.1 eq.103
  2.2 0.1 copy.15
  2.3 0.1 eq.108
  2.4 0.1 fusion
  2.5 0.1 concatenate.7
  2.6 0.6 convert_element_type.3.masks
  3.3 74.5 %shard_map.64 = f32[64,32,1024]{2,1,0:T(8,128)} custom-call(f32[64,32,1024]{2,1,0:T(8,128)} %f_hbm.1, f32[8,2048]{1,0:T(8,128)} %convert_element_type.3.masks, bf16[120,1024]{1,0:T(8,128)(2,1)} %constant.16.clone.w_ref, bf16[96,1152]{1,0:T(8,128)(2,1)} %constant.17.clone.b_ref, f32[8,128]{1,0:T(8,128)} %constant.18.clone.vec), custom_call_target="tpu_custom_call" | custom-call | tf_op jit(solution)/shard_map/pallas_call | solution.py:377
  77.7 8.4 %copy.18 = f32[64,32,1024]{2,1,0:T(8,128)} copy(f32[64,32,1024]{2,1,0:T(8,128)} %shard_map.64) | data formatting | bytes 16777216
  (1 shorter events, 0.0 us)

commit v2 on v1

--- a/solution.py
+++ b/solution.py
@@ -91,9 +91,85 @@
     return w, bst, vec, wall_norm, wall, norm
 
 
+def lanes_of(vec):
+    up = jnp.broadcast_to(vec[5:6, :], (8, LANES)) > 0.5
+    sub = lax.broadcasted_iota(jnp.int32, (8, LANES), 0)
+    return up, up & (sub == 0), jnp.logical_not(up) & (sub == 7)
+
+
+def relax(geometry, src, dst, dst_first, pst, b_ref, vec, sz, hr, bc, halves, before, after, dot_rows):
+    chunk, cols, nz, nch, sides = geometry
+    cc = chunk * cols
+    up, edge_lo, edge_hi = lanes_of(vec)
+
+    def spread(k, slot):
+        at = pl.ds(pl.multiple_of(k * cc, cc), cc)
+        bc[slot] = lax.dot_general(pst[:, at], b_ref[...], (((0,), (0,)), ((), ())),
+                                   preferred_element_type=F32)
+
+    def rows_of(k, slot):
+        for r in range(chunk):
+            i = k * chunk + r
+
+            def take(n):
+                return bc[slot, r * cols : (r + 1) * cols, n * LANES : (n + 1) * LANES]
+
+            inv_b = take(2 + nz)
+            for half in range(2):
+                exy = jnp.exp(take(half))
+                pxy = take(3 + nz + half)
+                for z in range(nz):
+                    b = 2 * z + half
+                    ln = slice(b * LANES, (b + 1) * LANES)
+                    c = src[1 + i, :, ln]
+                    side = src[i if half == 1 else i + 2, :, ln]
+                    dn = pltpu.roll(c, 1, 0)
+                    un = pltpu.roll(c, cols - 1, 0)
+                    hrow = jnp.broadcast_to(hr[0, k, r : r + 1, ln], (8, LANES))
+                    if sides == 2:
+                        hrow = jnp.where(up, hrow, jnp.broadcast_to(hr[1, k, r : r + 1, ln], (8, LANES)))
+                    s = []
+                    for t in range(cols // 8):
+                        tl = slice(8 * t, 8 * t + 8)
+                        v = jnp.where(up, dn[tl], un[tl])
+                        if t == 0:
+                            v = jnp.where(edge_lo, hrow, v)
+                        if t == cols // 8 - 1:
+                            v = jnp.where(edge_hi, hrow, v)
+                        s.append(v)
+                    s = jnp.concatenate(s, axis=0)
+                    moved = c * vec[half : half + 1, :] + side * vec[2 + half : 3 + half, :] + s * vec[4:5, :]
+                    new = inv_b * (moved + pxy * sz[z]) + take(2 + z) * exy
+                    dst[dst_first + i, :, ln] = new
+                    if halves is not None:
+                        hi = new.astype(BF16)
+                        halves[slot, 0, r * cols : (r + 1) * cols, ln] = hi
+                        halves[slot, 1, r * cols : (r + 1) * cols, ln] = (new - hi.astype(F32)).astype(BF16)
+
+    spread(0, 0)
+
+    def trip(m, carry):
+        k = 2 * m
+        before(k)
+        spread(k + 1, 1)
+        rows_of(k, 0)
+        if dot_rows is not None:
+            dot_rows(k, 0)
+        before(k + 1)
+        spread(lax.rem(k + 2, nch), 0)
+        rows_of(k + 1, 1)
+        if dot_rows is not None:
+            dot_rows(k + 1, 1)
+        after(k)
+        after(k + 1)
+        return carry
+
+    lax.fori_loop(0, nch // 2, trip, 0)
+
+
 def kernel(
-    cfg, f_hbm, masks, w_ref, b_ref, vec, out_hbm,
-    fa, fb, bc, q, qy, qx, a_ref, r_ref, p_ref, pst, hs, hr, hb, wold,
+    cfg, f_hbm, code, w_ref, b_ref, vec, f_mid, pst_out, hr_out, sz_out,
+    fa, fb, bc, q, qy, qx, a_ref, r_ref, p_ref, pst, hs, hr, halves, wold, masks,
     lsem, osem, zss, zrs, xss, xrs, hss, hrs, qyss, qyrs, qxss, qxrs,
 ):
     rows, cols, nz, nx, ny, nv, wall_norm, wall, norm = cfg
@@ -101,6 +177,7 @@
     chunk = 8
     cc = chunk * cols
     nch = rows // chunk
+    sides = 1 if ny == 2 else 2
     gx, gy, vt = lax.axis_index("gx"), lax.axis_index("gy"), lax.axis_index("vert")
     right, left = {"gx": lax.rem(gx + 1, nx)}, {"gx": lax.rem(gx + nx - 1, nx)}
     across = [{"gy": lax.rem(gy + 1, ny)}]
@@ -141,19 +218,22 @@
     z0 = (vt.astype(F32) * nz + (nz - 1) / 2.0 - (NVEL - 1) / 2.0) * H
     vz = [z0 + (z - (nz - 1) / 2.0) * H for z in range(nz)]
     sz = [jnp.exp(jnp.full((1, LANES), 0.0, F32) - vz[z] * vz[z] / (2 * WALL_T)) for z in range(nz)]
-    up = jnp.broadcast_to(vec[5:6, :], (8, LANES)) > 0.5
-    sub = lax.broadcasted_iota(jnp.int32, (8, LANES), 0)
-    edge_lo = up & (sub == 0)
-    edge_hi = jnp.logical_not(up) & (sub == 7)
-
-    def moments(x, k):
-        hi = x.astype(BF16)
-        lo = (x - hi.astype(F32)).astype(BF16)
+    up = lanes_of(vec)[0]
+
+    def moments(hi, lo, k):
         dims = (((1,), (1,)), ((), ()))
         o = lax.dot_general(w_ref[...], hi, dims, preferred_element_type=F32)
         o = o + lax.dot_general(w_ref[...], lo, dims, preferred_element_type=F32)
         at = pl.ds(pl.multiple_of(k * cc, cc), cc)
         q[:, at] = o[0:40] + o[40:80] + o[80:120]
+
+    def dot_rows(k, slot):
+        moments(halves[slot, 0], halves[slot, 1], k)
+
+    def mid_copy(buf, k):
+        return pltpu.make_async_copy(
+            buf.at[pl.ds(1 + k * chunk, chunk)], f_mid.at[pl.ds(1 + k * chunk, chunk)], osem.at[k]
+        )
 
     def pack(step, buf, k):
         for r in range(chunk):
@@ -167,7 +247,8 @@
     def load_chunk(k, carry):
         local_copy(k).wait()
         x = fa[pl.ds(1 + k * chunk, chunk)].reshape(cc, nz * PLANE)
-        moments(x, k)
+        hi = x.astype(BF16)
+        moments(hi, (x - hi.astype(F32)).astype(BF16), k)
         at = pl.ds(pl.multiple_of(k * cc, cc), cc)
         ones = (lax.broadcasted_iota(jnp.int32, (8, LANES), 0) == 0).astype(BF16)
         gasb = lax.dot_general(masks[:, at].astype(BF16), ones, (((0,), (0,)), ((), ())),
@@ -179,11 +260,17 @@
         pack(0, fa, k)
         return carry
 
+    flat = lax.broadcasted_iota(jnp.int32, (1, cells), 1)
+    for n, on in enumerate([code[...] == 0] + [code[...] == k + 1 for k in range(4)]
+                           + [code[...] > 0, flat % cols == 0, flat % cols == cols - 1]):
+        masks[n : n + 1, :] = jnp.where(on, 1.0, 0.0)
     xs = halo_x(0, f_hbm, 0, fa)
     for c in xs:
         c.start()
     lax.fori_loop(0, nch, load_chunk, 0)
 
+    first_col = masks[6:7, :] > 0.5
+    last_col = masks[7:8, :] > 0.5
     gas = masks[0:1, :]
     picks = [masks[1 + k : 2 + k, :] for k in range(4)]
     solid = masks[5:6, :] > 0.5
@@ -213,7 +300,7 @@
         for c in hcopy:
             c.start()
         if step > 0:
-            xs = halo_x(step, src, 1, src)
+            xs = halo_x(step, src, 1, f_mid if last else src)
             for c in xs:
                 c.start()
 
@@ -230,9 +317,8 @@
         right_in = jnp.concatenate([pltpu.roll(qx[step, 1], LANES - cols, 1)] * reps, axis=1)
         sxp = jnp.where(lane < cols, left_in, sxp)
         sxm = jnp.where(lane >= cells - cols, right_in, sxm)
-        col = lane % cols
-        syp = jnp.where(col == 0, shift(qy[step, 0, 0:8], 1 - cols), syp)
-        sym = jnp.where(col == cols - 1, shift(qy[step, len(across) - 1, 8:16], cols - 1), sym)
+        syp = jnp.where(first_col, shift(qy[step, 0, 0:8], 1 - cols), syp)
+        sym = jnp.where(last_col, shift(qy[step, len(across) - 1, 8:16], cols - 1), sym)
         part = base + COURANT * (sxp + sxm + syp + sym)
         z_row = part[3:4] + z0 * part[0:1]
         e_row = part[4:5] + 2 * z0 * part[3:4] + z0 * z0 * part[0:1]
@@ -286,72 +372,52 @@
 
         for c in hcopy + xs:
             c.wait()
-
-        def relax_row(i, rr, bcrow):
-            def take(n):
-                return bc[pl.ds(bcrow, cols), n * LANES : (n + 1) * LANES]
-
-            inv_b = take(2 + nz)
-            for half in range(2):
-                exy = jnp.exp(take(half))
-                pxy = take(3 + nz + half)
-                for z in range(nz):
-                    b = 2 * z + half
-                    ln = slice(b * LANES, (b + 1) * LANES)
-                    c = src[1 + i, :, ln]
-                    r = src[i if half == 1 else i + 2, :, ln]
-                    dn = pltpu.roll(c, 1, 0)
-                    un = pltpu.roll(c, cols - 1, 0)
-                    hrow = hb[rr, :, ln]
-                    s = []
-                    for t in range(cols // 8):
-                        tl = slice(8 * t, 8 * t + 8)
-                        v = jnp.where(up, dn[tl], un[tl])
-                        if t == 0:
-                            v = jnp.where(edge_lo, hrow, v)
-                        if t == cols // 8 - 1:
-                            v = jnp.where(edge_hi, hrow, v)
-                        s.append(v)
-                    s = jnp.concatenate(s, axis=0)
-                    moved = c * vec[half : half + 1, :] + r * vec[2 + half : 3 + half, :] + s * vec[4:5, :]
-                    dst[1 + i, :, ln] = inv_b * (moved + pxy * sz[z]) + take(2 + z) * exy
-
-        def out_copy(k):
-            return pltpu.make_async_copy(
-                dst.at[pl.ds(1 + k * chunk, chunk)], out_hbm.at[pl.ds(k * chunk, chunk)], osem.at[k]
-            )
-
-        def relax_chunk(k, carry):
-            at = pl.ds(pl.multiple_of(k * cc, cc), cc)
-            bc[...] = lax.dot_general(pst[:, at], b_ref[...], (((0,), (0,)), ((), ())),
-                                      preferred_element_type=F32)
-
-            def one(r, c2):
-                relax_row(k * chunk + r, r, pl.multiple_of(r * cols, cols))
-                return c2
-
-            for r in range(chunk):
-                for b in range(2 * nz):
-                    ln = slice(b * LANES, (b + 1) * LANES)
-                    low = jnp.broadcast_to(hr[step, 0, k, r : r + 1, ln], (8, LANES))
-                    if ny == 2:
-                        hb[r, :, ln] = low
-                    else:
-                        high = jnp.broadcast_to(hr[step, 1, k, r : r + 1, ln], (8, LANES))
-                        hb[r, :, ln] = jnp.where(up, low, high)
-
-            lax.fori_loop(0, chunk, one, 0)
-            if last:
-                out_copy(k).start()
-            else:
-                pack(step + 1, dst, k)
-                moments(dst[pl.ds(1 + k * chunk, chunk)].reshape(cc, nz * PLANE), k)
-            return carry
-
-        lax.fori_loop(0, nch, relax_chunk, 0)
         if last:
-            for k in range(nch):
-                out_copy(k).wait()
+            break
+
+        def before(k):
+            return None
+
+        def after(k, step=step, dst=dst):
+            pack(step + 1, dst, k)
+            if step == STEPS - 2:
+                mid_copy(dst, k).start()
+
+        relax((chunk, cols, nz, nch, sides), src, dst, 1, pst, b_ref, vec, sz, hr.at[step],
+              bc, halves, before, after, dot_rows)
+    for k in range(nch):
+        mid_copy(bufs[(STEPS - 1) % 2], k).wait()
+    pst_out[...] = pst[...]
+    hr_out[...] = hr[STEPS - 1]
+    for z in range(nz):
+        sz_out[z : z + 1, :] = sz[z]
+    for z in range(nz, 8):
+        sz_out[z : z + 1, :] = jnp.zeros((1, LANES), F32)
+
+
+def finish(geometry, rows, f_mid, pst, hr, sz_ref, b_ref, vec, out_hbm, fa, fb, bc, lsem, osem):
+    chunk, cols, nz, nch, sides = geometry
+
+    def part(k):
+        return pltpu.make_async_copy(
+            f_mid.at[pl.ds(2 + k * chunk, chunk)], fa.at[pl.ds(2 + k * chunk, chunk)], lsem.at[k]
+        )
+
+    def out_copy(k):
+        return pltpu.make_async_copy(
+            fb.at[pl.ds(k * chunk, chunk)], out_hbm.at[pl.ds(k * chunk, chunk)], osem.at[k]
+        )
+
+    first = pltpu.make_async_copy(f_mid.at[pl.ds(0, 2)], fa.at[pl.ds(0, 2)], lsem.at[nch])
+    first.start()
+    for k in range(nch):
+        part(k).start()
+    first.wait()
+    sz = [sz_ref[z : z + 1, :] for z in range(nz)]
+    relax(geometry, fa, fb, 0, pst, b_ref, vec, sz, hr, bc, None,
+          lambda k: part(k).wait(), lambda k: out_copy(k).start(), None)
+    for k in range(nch):
+        out_copy(k).wait()
 
 
 def solution(mesh):
@@ -363,26 +429,30 @@
         nz = vel // PLANE
         cells = rows * cols
         w, bst, vec, wall_norm, wall, norm = tables(nz)
-        sm = solid_mask.reshape(1, cells) == 1
-        nc = normal_code.reshape(1, cells)
-        lines = [jnp.logical_not(sm)] + [sm & (nc == k) for k in range(4)] + [sm]
-        lines += [jnp.zeros_like(sm)] * 2
-        masks = jnp.concatenate(lines, axis=0).astype(F32)
+        code = jnp.where(solid_mask == 1, normal_code + 1, 0).reshape(1, cells)
+        nch = rows // 8
+        geometry = (8, cols, nz, nch, sides)
         cfg = (rows, cols, nz, nx, ny, nv, wall_norm, wall, norm)
         vm = pl.BlockSpec(memory_space=pltpu.VMEM)
         hbm = pl.BlockSpec(memory_space=pl.ANY)
         dma = pltpu.SemaphoreType.DMA
         bw = bst.shape[1]
         chunk = 8
-        return pl.pallas_call(
+        bst, vec = jnp.asarray(bst), jnp.asarray(vec)
+        f_mid, pst, hr, sz = pl.pallas_call(
             functools.partial(kernel, cfg),
-            out_shape=jax.ShapeDtypeStruct(f.shape, F32),
+            out_shape=[
+                jax.ShapeDtypeStruct((rows + 2, cols, vel), F32),
+                jax.ShapeDtypeStruct((96, cells), BF16),
+                jax.ShapeDtypeStruct((sides, nch, chunk, vel), F32),
+                jax.ShapeDtypeStruct((8, LANES), F32),
+            ],
             in_specs=[hbm, vm, vm, vm, vm],
-            out_specs=hbm,
+            out_specs=[pl.BlockSpec(memory_space=pltpu.HBM), vm, vm, vm],
             scratch_shapes=[
                 pltpu.VMEM((rows + 2, cols, vel), F32),
                 pltpu.VMEM((rows + 2, cols, vel), F32),
-                pltpu.VMEM((chunk * cols, bw), F32),
+                pltpu.VMEM((2, chunk * cols, bw), F32),
                 pltpu.VMEM((40, cells), F32),
                 pltpu.VMEM((STEPS, sides, 16, cells), F32),
                 pltpu.VMEM((STEPS, 2, 8, LANES), F32),
@@ -392,8 +462,9 @@
                 pltpu.VMEM((96, cells), BF16),
                 pltpu.VMEM((STEPS, rows // chunk, chunk, vel), F32),
                 pltpu.VMEM((STEPS, sides, rows // chunk, chunk, vel), F32),
-                pltpu.VMEM((chunk, 8, vel), F32),
+                pltpu.VMEM((2, 2, chunk * cols, vel), BF16),
                 pltpu.VMEM((1, cells), F32),
+                pltpu.VMEM((8, cells), F32),
                 dma((rows // chunk,)), dma((rows // chunk,)),
                 dma((STEPS, nv - 1)), dma((STEPS, nv - 1)),
                 dma((STEPS, 2, nz)), dma((STEPS, 2, nz)),
@@ -404,7 +475,20 @@
             compiler_params=pltpu.CompilerParams(
                 collective_id=0, has_side_effects=True, vmem_limit_bytes=60 * 2**20
             ),
-        )(f, masks, jnp.asarray(w), jnp.asarray(bst), jnp.asarray(vec))
+        )(f, code, jnp.asarray(w), bst, vec)
+        return pl.pallas_call(
+            functools.partial(finish, geometry, rows),
+            out_shape=jax.ShapeDtypeStruct(f.shape, F32),
+            in_specs=[pl.BlockSpec(memory_space=pltpu.HBM), vm, vm, vm, vm, vm],
+            out_specs=hbm,
+            scratch_shapes=[
+                pltpu.VMEM((rows + 2, cols, vel), F32),
+                pltpu.VMEM((rows, cols, vel), F32),
+                pltpu.VMEM((2, chunk * cols, bw), F32),
+                dma((nch + 1,)), dma((nch,)),
+            ],
+            compiler_params=pltpu.CompilerParams(vmem_limit_bytes=60 * 2**20),
+        )(f_mid, pst, hr, sz, bst, vec)
 
     placed = (P("gx", "gy", "vert"), P("gx", "gy"), P("gx", "gy"))
     return jax.shard_map(

time: 86.5 us -> 73.5 us (0.85)
  local copies, waits for them, and re-layouts: 9.51 us -> 0.77 us
  Pallas kernels: 74.5 us -> 71.6 us
  other arithmetic: 2.15 us -> 0.74 us
    unnamed x1 -> x0, local copies, waits for them, and re-layouts: 8.44 us -> none
    pallas_call x1 -> x2, Pallas kernels: 74.5 us -> 71.6 us  [the longest x1 60.7 us: on_device(): pl.pallas_call(functools.partial(kernel, cfg), out_shape=[jax.ShapeDtypeS...]
    eq x2 -> x0, other arithmetic: 1.46 us -> none  [the longest x1 0.73 us: on_device(): lines = [jnp.logical_not(sm)] + [sm & (nc == k) for k in range(4)] + [sm]]
    eq x10 -> x0, local copies, waits for them, and re-layouts: 0.96 us -> none  [the longest x8 0.77 us: on_device(): lines = [jnp.logical_not(sm)] + [sm & (nc == k) for k in range(4)] + [sm]]
where the time goes in v2:
time: 73.5 us; the launch traced here: 73.1 us
  Pallas kernels  71.6 us (97%)
  local copies, waits for them, and re-layouts  0.77 us (1%)
  other arithmetic  0.74 us (1%)
    pallas_call x1, Pallas kernels, on_device(): pl.pallas_call(functools.partial(kernel, cfg), out_shape=[jax.ShapeDtypeS...  60.7 us
    pallas_call x1, Pallas kernels, on_device(): pl.pallas_call(functools.partial(finish, geometry, rows), out_shape=jax.S...  10.9 us

profile of v2, /device:TPU:0, one launch (start us, length us, event | category | flops | bytes accessed | tf_op | source)
XLA Modules:
  0.0 73.1 jit_solution(14389236859990435196)
XLA Ops:
  0.0 0.7 %add_select_fusion = s32[64,32]{0,1:T(8,128)S(1)} fusion(s32[64,32]{0,1:T(8,128)} %param.8, s32[64,32]{0,1:T(8,128)} %param.7), kind=kLoop, calls=%fused_computation | loop fusion | flops 6144 | bytes 24576 | tf_op jit(solution)/shard_map/jit(_where)/select_n | solution.py:432
  0.7 0.1 copy.8
  0.8 0.7 reshape.3.code
  1.5 60.7 %shard_map.64 = (f32[66,32,1024]{2,1,0:T(8,128)}, bf16[96,2048]{1,0:T(8,128)(2,1)}, f32[1,8,8,1024]{3,2,1,0:T(8,128)}, f32[8,128]{1,0:T(8,128)}) custom-call(f32[64,32,1024]{2,1,0:T(8,128)} %f_hbm.1, s32[1,2048]{1,0:T(1,128)} %reshape.3.code, bf16[120,1024]{1,0:T(8,128)(2,1)} %constant.12.clone.w_ref, bf16[96,1152]{1,0:T(8,128)(2,1)} %constant.10.clone.b_ref, ...), custom_call_target="tpu_custom_call" | custom-call | tf_op jit(solution)/shard_map/pallas_call | solution.py:442
  62.2 10.9 %shard_map.65 = f32[64,32,1024]{2,1,0:T(8,128)} custom-call(f32[66,32,1024]{2,1,0:T(8,128)} %get-tuple-element.9.f_mid, bf16[96,2048]{1,0:T(8,128)(2,1)} %get-tuple-element.10.pst, f32[1,8,8,1024]{3,2,1,0:T(8,128)} %get-tuple-element.11.hr, f32[8,128]{1,0:T(8,128)} %get-tuple-element.12.sz_ref, bf16[96,1152]{1,0:T(8,128)(2,1)} %constant.10.clone.b_ref, ...), custom_call_target="tpu_custom_call" | custom-call | tf_op jit(solution)/shard_map/pallas_call | solution.py:479

commit v3 on v2

--- a/solution.py
+++ b/solution.py
@@ -324,16 +324,16 @@
         e_row = part[4:5] + 2 * z0 * part[3:4] + z0 * z0 * part[0:1]
         part = jnp.where(row8 == 3, z_row, jnp.where(row8 == 4, e_row, jnp.where(row8 == 5, inc, part)))
         a_ref[...] = part
-        zc = [remote(a_ref, r_ref.at[step, k], zss.at[step, k], zrs.at[step, k], peers[k])
+        zc = [remote(a_ref.at[pl.ds(0, 6)], r_ref.at[step, k, pl.ds(0, 6)], zss.at[step, k], zrs.at[step, k], peers[k])
               for k in range(nv - 1)]
         for c in zc:
             c.start()
         for c in zc:
             c.wait()
-        tot = part
+        tot = part[0:6]
         for k in range(nv - 1):
-            tot = tot + r_ref[step, k]
-        p_ref[0:8, :] = tot
+            tot = tot + r_ref[step, k, 0:6]
+        p_ref[0:6, :] = tot
         w = p_ref[5:6, :] * (1.0 / wall_norm)
         near = [shift(w, cols), shift(w, -cols), shift(w, 1), shift(w, -1)]
         mom = []

time: 73.5 us -> 71.7 us (0.976)
  Pallas kernels: 71.6 us -> 69.8 us
    pallas_call x1, Pallas kernels: 60.7 us -> 58.9 us  [on_device(): pl.pallas_call(functools.partial(kernel, cfg), out_shape=[jax.ShapeDtypeS...]
where the time goes in v3:
time: 71.7 us; the launch traced here: 71.3 us
  Pallas kernels  69.8 us (97%)
  local copies, waits for them, and re-layouts  0.77 us (1%)
  other arithmetic  0.74 us (1%)
    pallas_call x1, Pallas kernels, on_device(): pl.pallas_call(functools.partial(kernel, cfg), out_shape=[jax.ShapeDtypeS...  58.9 us
    pallas_call x1, Pallas kernels, on_device(): pl.pallas_call(functools.partial(finish, geometry, rows), out_shape=jax.S...  10.9 us

profile of v3, /device:TPU:0, one launch (start us, length us, event | category | flops | bytes accessed | tf_op | source)
XLA Modules:
  0.0 71.3 jit_solution(2389596098839439881)
XLA Ops:
  0.0 0.7 %add_select_fusion = s32[64,32]{0,1:T(8,128)S(1)} fusion(s32[64,32]{0,1:T(8,128)} %param.8, s32[64,32]{0,1:T(8,128)} %param.7), kind=kLoop, calls=%fused_computation | loop fusion | flops 6144 | bytes 24576 | tf_op jit(solution)/shard_map/jit(_where)/select_n | solution.py:432
  0.7 0.1 copy.8
  0.8 0.7 reshape.3.code
  1.5 58.9 %shard_map.64 = (f32[66,32,1024]{2,1,0:T(8,128)}, bf16[96,2048]{1,0:T(8,128)(2,1)}, f32[1,8,8,1024]{3,2,1,0:T(8,128)}, f32[8,128]{1,0:T(8,128)}) custom-call(f32[64,32,1024]{2,1,0:T(8,128)} %f_hbm.1, s32[1,2048]{1,0:T(1,128)} %reshape.3.code, bf16[120,1024]{1,0:T(8,128)(2,1)} %constant.12.clone.w_ref, bf16[96,1152]{1,0:T(8,128)(2,1)} %constant.10.clone.b_ref, ...), custom_call_target="tpu_custom_call" | custom-call | tf_op jit(solution)/shard_map/pallas_call | solution.py:442
  60.4 10.9 %shard_map.65 = f32[64,32,1024]{2,1,0:T(8,128)} custom-call(f32[66,32,1024]{2,1,0:T(8,128)} %get-tuple-element.9.f_mid, bf16[96,2048]{1,0:T(8,128)(2,1)} %get-tuple-element.10.pst, f32[1,8,8,1024]{3,2,1,0:T(8,128)} %get-tuple-element.11.hr, f32[8,128]{1,0:T(8,128)} %get-tuple-element.12.sz_ref, bf16[96,1152]{1,0:T(8,128)(2,1)} %constant.10.clone.b_ref, ...), custom_call_target="tpu_custom_call" | custom-call | tf_op jit(solution)/shard_map/pallas_call | solution.py:479
